TPU v7x, 256 devices: a whole 4x4x8 slice. The times are simulated.
256 devices in a mesh: row: 16 (over x, y), col: 16 (over z, core).
Axes of the slice: x: 4, y: 4, z: 8, core: 2. Of those that a mesh axis runs over, the one named last changes fastest.
Arguments:
- trailing_slab: float32 [131072, 2048], P('row', 'col'), may hold values from -6 to 6, as said below
- panel_columns: float32 [32, 131072], P(None, 'row'), may hold values from -1870.1934 to 1870.1934
- far_image: float32 [32, 131072], P(None, 'row'), may hold values from -2048 to 2048
Outputs:
- updated_slab: float32 [131072, 2048], P('row', 'col')
- update_factor: float32 [32, 131072], P(None, 'row')
Inputs may be any that keep to these rules, and one draw needn't show every extreme that they name: Rows 0 to 2047 of trailing_slab form a symmetric block.
All inputs are finite; a program needn't handle non-finite values.
Results may differ from a plain program's by a relative error of at most 0.0003.
Values sent between devices are 32-bit elements; how exact they have to be, the bound alone decides.
A program may use at most 64 MiB of HBM per device.

v0:
```python
import jax
import jax.numpy as jnp
from jax import lax
from jax.sharding import PartitionSpec as P


def from_root(block, axis, owner):
    block = jnp.where(lax.axis_index(axis) == owner, block, jnp.zeros_like(block))
    return lax.psum(block, axis)


def product(left, right):
    return jnp.dot(left, right, precision=lax.Precision.HIGHEST, preferred_element_type=jnp.float32)


def contract(left, right, left_dim, right_dim):
    return lax.dot_general(
        left,
        right,
        (((left_dim,), (right_dim,)), ((), ())),
        precision=lax.Precision.HIGHEST,
        preferred_element_type=jnp.float32,
    )


def cholesky_rows(gram_total):
    panel_width = gram_total.shape[0]
    identity = jnp.eye(panel_width, dtype=jnp.float32)
    indices = jnp.arange(panel_width)
    lower_part = jnp.zeros((panel_width, panel_width), jnp.float32)
    for column in range(panel_width):
        onehot = identity[column]
        residue = gram_total[:, column] - product(lower_part, lower_part[column])
        pivot = jnp.sqrt(jnp.sum(residue * onehot))
        new_column = jnp.where(indices >= column, residue / pivot, 0.0)
        lower_part = lower_part + new_column[:, None] * onehot[None, :]
    return lower_part


def invert_lower(lower_part):
    panel_width = lower_part.shape[0]
    identity = jnp.eye(panel_width, dtype=jnp.float32)
    inverse = jnp.zeros((panel_width, panel_width), jnp.float32)
    for index_row in range(panel_width):
        onehot = identity[index_row]
        pivot = jnp.sum(lower_part[index_row] * onehot)
        new_row = (onehot - product(lower_part[index_row], inverse)) / pivot
        inverse = inverse + onehot[:, None] * new_row[None, :]
    return inverse


def decompose(shifted):
    panel_width = shifted.shape[0]
    identity = jnp.eye(panel_width, dtype=jnp.float32)
    indices = jnp.arange(panel_width)
    lower_unit = identity
    upper_part = shifted
    for column in range(panel_width):
        factor = jnp.where(
            indices > column, upper_part[:, column] / upper_part[column, column], 0.0
        )
        lower_unit = lower_unit + factor[:, None] * identity[column][None, :]
        upper_part = upper_part - factor[:, None] * upper_part[column][None, :]
    return (lower_unit, jnp.triu(upper_part))


def factors(gram_total, top_rows):
    panel_width = gram_total.shape[0]
    identity = jnp.eye(panel_width, dtype=jnp.float32)
    cholesky_lower = cholesky_rows(gram_total)
    cholesky_inverse = invert_lower(cholesky_lower)
    top_factor = product(cholesky_inverse, top_rows).T
    sign_flip = jnp.where(jnp.diag(top_factor) >= 0.0, -1.0, 1.0).astype(jnp.float32)
    lower_unit, upper_part = decompose(identity - top_factor * sign_flip[None, :])
    upper_inverse = invert_lower(upper_part.T).T
    root_inverse = cholesky_inverse.T
    mixing = -product(root_inverse * sign_flip[None, :], upper_inverse)
    lower_inverse = invert_lower(lower_unit)
    triangle = product(upper_part, lower_inverse.T)
    return (mixing, upper_inverse, triangle)


def local(trailing_slab, panel_columns, far_image):
    cols_dev = trailing_slab.shape[1]
    panel_width = panel_columns.shape[0]
    row_pos = lax.axis_index("row")
    col_pos = lax.axis_index("col")
    top_row = row_pos == 0
    gram_part = product(panel_columns, panel_columns.T)
    top_local = panel_columns[:, :panel_width]
    gram_total = lax.psum(gram_part, "row")
    top_rows = from_root(top_local, "row", 0)
    mixing, upper_inverse, triangle = factors(gram_total, top_rows)
    reflectors = product(mixing.T, panel_columns)
    head_rows = jnp.where(top_row, upper_inverse.T, 0.0)
    reflectors = reflectors.at[:, :panel_width].add(head_rows)
    col_start = col_pos * cols_dev
    own_reflectors = from_root(
        lax.dynamic_slice_in_dim(reflectors, col_start, cols_dev, 1), "row", 0
    )
    far_part = product(mixing.T, far_image)
    local_image = contract(own_reflectors, trailing_slab, 1, 1)
    images = lax.psum(local_image, "col") + far_part
    inner_block = lax.psum(product(reflectors, images.T), "row")
    core_block = product(product(triangle.T, inner_block), triangle)
    weights = product(triangle.T, images) - 0.5 * product(core_block.T, reflectors)
    own_weights = from_root(lax.dynamic_slice_in_dim(weights, col_start, cols_dev, 1), "row", 0)
    updated = (
        trailing_slab
        - contract(reflectors, own_weights, 0, 0)
        - contract(weights, own_reflectors, 0, 0)
    )
    return (updated, weights)


def solution(mesh):
    in_specs = (P("row", "col"), P(None, "row"), P(None, "row"))
    out_specs = (P("row", "col"), P(None, "row"))
    return jax.shard_map(local, mesh=mesh, in_specs=in_specs, out_specs=out_specs, check_vma=False)
```

profile of v0, /device:TPU:0, one launch (start us, length us, event | category | flops | bytes accessed | tf_op | source)
XLA Modules:
  0.0 674.5 jit_solution(5860183124567604668)
XLA Ops:
  9.0 2.6 fusion.969
  12.3 72.9 %all-reduce = (f32[32,32]{0,1:T(8,128)S(1)}, f32[32,32]{1,0:T(8,128)S(1)}) all-reduce(f32[32,32]{0,1:T(8,128)S(1)} %broadcast_select_fusion, f32[32,32]{1,0:T(8,128)S(1)} %fusion.969), channel_id=1, replica_groups=mesh['row'=16,'col'=16] {'row'}, use_global_device_ids=true, to_apply=%region_65.66 | all-reduce | flops 2048 | bytes 16384 | tf_op jit(solution)/shard_map/psum | solution.py:9
  166.8 0.9 fusion.131
  171.0 0.9 fusion.136
  171.9 0.9 fusion.137
  172.8 0.9 fusion.138
  174.5 0.9 fusion.140
  181.4 0.9 fusion.148
  183.2 0.9 fusion.150
  191.8 0.9 fusion.160
  250.8 0.9 fusion.195
  253.2 0.9 fusion.197
  255.6 0.9 fusion.199
  258.0 0.9 fusion.201
  260.3 0.9 fusion.203
  267.9 0.9 fusion.168
  268.8 0.9 fusion.169
  269.7 1.0 fusion.170
  270.7 0.9 fusion.171
  271.6 0.9 fusion.172
  274.0 0.9 fusion.206
  276.4 0.9 fusion.208
  279.6 0.9 fusion.176
  282.1 0.9 fusion.178
  286.0 0.9 fusion.210
  287.8 0.9 fusion.212
  290.1 0.9 fusion.182
  294.1 0.9 fusion.214
  295.8 0.9 fusion.216
  298.2 0.9 fusion.186
  302.1 0.9 fusion.218
  303.8 0.9 fusion.220
  306.3 0.9 fusion.190
  308.5 0.9 fusion.192
  309.9 1.2 fusion.970
  312.4 69.5 %psum.44 = f32[32,128]{1,0:T(8,128)S(1)} all-reduce(f32[32,128]{1,0:T(8,128)S(1)} %dynamic-slice_select_fusion.1), channel_id=1, replica_groups=mesh['row'=16,'col'=16] {'row'}, use_global_device_ids=true, to_apply=%region_131.132 | all-reduce | flops 4096 | bytes 32768 | tf_op jit(solution)/shard_map/psum | solution.py:9
  381.9 7.4 %fusion.971 = f32[32,8192]{1,0:T(8,128)} fusion(f32[32,128]{1,0:T(8,128)S(1)} %psum.44, f32[8192,128]{1,0:T(8,128)} %param.5), kind=kOutput, calls=%fused_computation.1690 | convolution fusion | flops 402653184 | bytes 5259264 | tf_op jit(solution)/shard_map/dot_general | solution.py:17
  390.0 0.9 fusion.222
  391.7 0.9 fusion.224
  392.9 105.8 %all-reduce.3.cloned.1.call-done = f32[32,8192]{1,0:T(8,128)} async-done(((f32[32,8192]{1,0:T(8,128)}), f32[32,8192]{1,0:T(8,128)}) %all-reduce.3.cloned.1.call-update) | async-done | bytes 1048592 | tf_op jit(solution)/shard_map/psum | solution.py:103
  498.7 2.3 convolution_add_fusion
  500.9 1.0 fusion.973
  501.9 2.0 fusion.972
  503.9 74.2 %psum.46 = f32[32,32]{1,0:T(8,128)S(1)} all-reduce(f32[32,32]{1,0:T(8,128)S(1)} %fusion.973), channel_id=1, replica_groups=mesh['row'=16,'col'=16] {'row'}, use_global_device_ids=true, to_apply=%region_133.134 | all-reduce | flops 1024 | bytes 8192 | tf_op jit(solution)/shard_map/psum | solution.py:104
  578.5 2.3 fusion
  580.9 69.7 %psum.47 = f32[32,128]{1,0:T(8,128)S(1)} all-reduce(f32[32,128]{1,0:T(8,128)S(1)} %dynamic-slice_select_fusion), channel_id=1, replica_groups=mesh['row'=16,'col'=16] {'row'}, use_global_device_ids=true, to_apply=%region_134.135 | all-reduce | flops 4096 | bytes 32768 | tf_op jit(solution)/shard_map/psum | solution.py:9
  650.6 8.5 %convolution_subtract_fusion.1 = f32[8192,128]{1,0:T(8,128)S(1)} fusion(f32[8192,128]{1,0:T(8,128)} %param.5, f32[32,8192]{1,0:T(8,128)S(1)} %scatter-add.4, f32[32,128]{1,0:T(8,128)S(1)} %psum.47), kind=kOutput, calls=%fused_computation.2 | convolution fusion | flops 403701760 | bytes 9453568 | tf_op jit(solution)/shard_map/dot_general | solution.py:17
  659.2 8.3 %convolution_subtract_fusion = f32[8192,128]{1,0:T(8,128)} fusion(f32[8192,128]{1,0:T(8,128)S(1)} %convolution_subtract_fusion.1, f32[32,8192]{1,0:T(8,128)S(1)} %fusion, f32[32,128]{1,0:T(8,128)S(1)} %psum.44), kind=kOutput, calls=%fused_computation.1 | convolution fusion | flops 403701760 | bytes 9453568 | tf_op jit(solution)/shard_map/dot_general | solution.py:17
  (419 shorter events, 179.0 us)
Async XLA Ops:
  7.2 491.5 %copy-start = (f32[32,8192]{1,0:T(8,128)S(1)}, f32[32,8192]{1,0:T(8,128)}, u32[]{:S(2)}) copy-start(f32[32,8192]{1,0:T(8,128)} %param.7) | copy-start | bytes 3145732
  7.2 491.5 %all-reduce.3.cloned.1.call-start = ((), (), s32[]{:S(2)}) async-start(), calls=%async_computation | async-start | bytes 2097152 | tf_op jit(solution)/shard_map/psum | solution.py:103
  269.7 40.2 %copy-start.1 = (f32[32,8192]{1,0:T(8,128)S(1)}, f32[32,8192]{1,0:T(8,128)}, u32[]{:S(2)}) copy-start(f32[32,8192]{1,0:T(8,128)} %param.6) | copy-start | bytes 3145732
  580.8 78.3 %copy-start.2 = (f32[32,8192]{1,0:T(8,128)}, f32[32,8192]{1,0:T(8,128)S(1)}, u32[]{:S(2)}) copy-start(f32[32,8192]{1,0:T(8,128)S(1)} %fusion) | copy-start | bytes 3145732
Sparse Core Ops, SparseCore 0:
  389.4 109.2 all-reduce.2
where the time goes:
time: 686 us; the launch traced here: 674 us
  blocking collectives  286 us (42%)
  matrix products  141 us (21%)
  waiting for transfers between devices  106 us (15%)
  other arithmetic  66 us (10%)
  between operations  37.7 us (5%)
  local copies, waits for them, and re-layouts  37.1 us (5%)
    psum x3, blocking collectives, from_root(): return lax.psum(block, axis)  212 us
    dot_general x139, matrix products, product(): jnp.dot(left, right, precision=lax.Precision.HIGHEST, preferred_element_t...  117 us
    psum x1, waiting for transfers between devices, local(): images = lax.psum(local_image, 'col') + far_part  106 us
    psum x1, blocking collectives, local(): inner_block = lax.psum(product(reflectors, images.T), 'row')  74.2 us
    reduce_sum x49, other arithmetic, invert_lower(): pivot = jnp.sum(lower_part[index_row] * onehot)  31.5 us
    dot_general x3, matrix products, contract(): lax.dot_general(left, right, (((left_dim,), (right_dim,)), ((), ())), pre...  24.2 us
    mul x32, other arithmetic, decompose(): upper_part = upper_part - factor[:, None] * upper_part[column][None, :]  21 us
    slice x32, local copies, waits for them, and re-layouts, decompose(): upper_part[column, column]  18.6 us
  transfers between devices with their start and end apart: 1, of which 1 were waited for; matrix products, arithmetic and copies ran while one was open for 1% of the time, Pallas kernels for 0%

commit v1 on v0

--- a/solution.py
+++ b/solution.py
@@ -6,7 +6,7 @@
 
 def from_root(block, axis, owner):
     block = jnp.where(lax.axis_index(axis) == owner, block, jnp.zeros_like(block))
-    return lax.psum(block, axis)
+    return jnp.sum(lax.all_gather(block, axis), axis=0)
 
 
 def product(left, right):

time: 686 us -> 616 us (0.90)
  the two profiles are of different devices: /device:TPU:0 before, /device:TPU:2 now
where the time goes in v1:
time: 616 us; the launch traced here: 605 us
  blocking collectives  213 us (35%)
  matrix products  141 us (23%)
  waiting for transfers between devices  111 us (18%)
  other arithmetic  66.1 us (11%)
  between operations  37.8 us (6%)
  local copies, waits for them, and re-layouts  36 us (6%)
    dot_general x139, matrix products, product(): jnp.dot(left, right, precision=lax.Precision.HIGHEST, preferred_element_t...  117 us
    psum x1, waiting for transfers between devices, local(): images = lax.psum(local_image, 'col') + far_part  111 us
    all_gather x3, blocking collectives, from_root(): return jnp.sum(lax.all_gather(block, axis), axis=0)  75.9 us
    psum x1, blocking collectives, local(): gram_total = lax.psum(gram_part, 'row')  68.5 us
    psum x1, blocking collectives, local(): inner_block = lax.psum(product(reflectors, images.T), 'row')  68.2 us
    reduce_sum x49, other arithmetic, invert_lower(): pivot = jnp.sum(lower_part[index_row] * onehot)  31.5 us
    dot_general x3, matrix products, contract(): lax.dot_general(left, right, (((left_dim,), (right_dim,)), ((), ())), pre...  24.2 us
    mul x32, other arithmetic, decompose(): upper_part = upper_part - factor[:, None] * upper_part[column][None, :]  21 us
  transfers between devices with their start and end apart: 1, of which 1 were waited for; matrix products, arithmetic and copies ran while one was open for 1% of the time, Pallas kernels for 0%

profile of v1, /device:TPU:2, one launch (start us, length us, event | category | flops | bytes accessed | tf_op | source)
XLA Modules:
  0.0 604.6 jit_solution(17532530433387737667)
XLA Ops:
  9.0 2.5 fusion.969
  11.5 68.5 %psum.21 = f32[32,32]{1,0:T(8,128)S(1)} all-reduce(f32[32,32]{1,0:T(8,128)S(1)} %fusion.969), channel_id=1, replica_groups=mesh['row'=16,'col'=16] {'row'}, use_global_device_ids=true, to_apply=%region_0.0 | all-reduce | flops 1024 | bytes 8192 | tf_op jit(solution)/shard_map/psum | solution.py:91
  161.6 0.9 fusion.131
  165.9 0.9 fusion.136
  166.8 0.9 fusion.137
  167.7 0.9 fusion.138
  169.4 0.9 fusion.140
  176.3 0.9 fusion.148
  178.1 0.9 fusion.150
  184.5 27.7 %all-gather = f32[512,32]{1,0:T(8,128)S(1)} all-gather(f32[32,32]{1,0:T(8,128)S(1)} %copy.14), channel_id=2, replica_groups=mesh['row'=16,'col'=16] {'row'}, dimensions={0}, use_global_device_ids=true | all-gather | bytes 69632 | tf_op jit(solution)/shard_map/all_gather | solution.py:9
  214.6 0.9 fusion.160
  273.2 0.9 fusion.195
  275.6 0.9 fusion.197
  278.0 0.9 fusion.199
  280.3 0.9 fusion.201
  282.7 0.9 fusion.203
  290.3 0.9 fusion.168
  291.2 0.9 fusion.169
  292.1 1.0 fusion.170
  293.0 0.9 fusion.171
  294.0 0.9 fusion.172
  296.4 0.9 fusion.206
  298.8 0.9 fusion.208
  302.0 0.9 fusion.176
  304.5 0.9 fusion.178
  308.4 0.9 fusion.210
  310.1 0.9 fusion.212
  312.5 0.9 fusion.182
  316.5 0.9 fusion.214
  318.2 0.9 fusion.216
  320.6 0.9 fusion.186
  322.9 1.0 fusion.188
  326.4 0.9 fusion.220
  331.1 0.9 fusion.192
  332.4 1.0 fusion.970
  334.7 20.7 %all-gather.1 = f32[512,128]{1,0:T(8,128)S(1)} all-gather(f32[32,128]{1,0:T(8,128)S(1)} %dynamic-slice_select_fusion.1), channel_id=3, replica_groups=mesh['row'=16,'col'=16] {'row'}, dimensions={0}, use_global_device_ids=true | all-gather | bytes 278528 | tf_op jit(solution)/shard_map/all_gather | solution.py:9
  355.4 7.4 %fusion.971 = f32[32,8192]{1,0:T(8,128)} fusion(f32[32,128]{1,0:T(8,128)S(1)} %reduce_sum.1308, f32[8192,128]{1,0:T(8,128)} %param.5), kind=kOutput, calls=%fused_computation.1690 | convolution fusion | flops 402653184 | bytes 5259264 | tf_op jit(solution)/shard_map/dot_general | solution.py:17
  363.5 0.9 fusion.222
  365.3 0.9 fusion.224
  366.5 110.5 %all-reduce.2.cloned.1.call-done = f32[32,8192]{1,0:T(8,128)} async-done(((f32[32,8192]{1,0:T(8,128)}), f32[32,8192]{1,0:T(8,128)}) %all-reduce.2.cloned.1.call-update) | async-done | bytes 1048592 | tf_op jit(solution)/shard_map/psum | solution.py:103
  477.0 2.3 convolution_add_fusion
  479.3 1.0 fusion.973
  480.2 2.0 fusion.972
  482.2 68.2 %psum.23 = f32[32,32]{1,0:T(8,128)S(1)} all-reduce(f32[32,32]{1,0:T(8,128)S(1)} %fusion.973), channel_id=1, replica_groups=mesh['row'=16,'col'=16] {'row'}, use_global_device_ids=true, to_apply=%region_133.134 | all-reduce | flops 1024 | bytes 8192 | tf_op jit(solution)/shard_map/psum | solution.py:104
  550.8 2.3 fusion
  553.1 27.5 %all-gather.2 = f32[512,128]{1,0:T(8,128)S(1)} all-gather(f32[32,128]{1,0:T(8,128)S(1)} %dynamic-slice_select_fusion), channel_id=4, replica_groups=mesh['row'=16,'col'=16] {'row'}, dimensions={0}, use_global_device_ids=true | all-gather | bytes 278528 | tf_op jit(solution)/shard_map/all_gather | solution.py:9
  580.7 8.5 %convolution_subtract_fusion.1 = f32[8192,128]{1,0:T(8,128)S(1)} fusion(f32[8192,128]{1,0:T(8,128)} %param.5, f32[32,8192]{1,0:T(8,128)S(1)} %scatter-add.4, f32[32,128]{1,0:T(8,128)S(1)} %reduce_sum.1309), kind=kOutput, calls=%fused_computation.2 | convolution fusion | flops 403701760 | bytes 9453568 | tf_op jit(solution)/shard_map/dot_general | solution.py:17
  589.2 8.3 %convolution_subtract_fusion = f32[8192,128]{1,0:T(8,128)} fusion(f32[8192,128]{1,0:T(8,128)S(1)} %convolution_subtract_fusion.1, f32[32,8192]{1,0:T(8,128)S(1)} %fusion, f32[32,128]{1,0:T(8,128)S(1)} %reduce_sum.1308), kind=kOutput, calls=%fused_computation.1 | convolution fusion | flops 403701760 | bytes 9453568 | tf_op jit(solution)/shard_map/dot_general | solution.py:17
  (425 shorter events, 178.8 us)
Async XLA Ops:
  7.2 469.8 %copy-start = (f32[32,8192]{1,0:T(8,128)S(1)}, f32[32,8192]{1,0:T(8,128)}, u32[]{:S(2)}) copy-start(f32[32,8192]{1,0:T(8,128)} %param.7) | copy-start | bytes 3145732
  7.2 469.8 %all-reduce.2.cloned.1.call-start = ((), (), s32[]{:S(2)}) async-start(), calls=%async_computation | async-start | bytes 2097152 | tf_op jit(solution)/shard_map/psum | solution.py:103
  100.6 83.8 %slice-start = ((f32[32,8192]{1,0:T(8,128)}), f32[32,32]{1,0:T(8,128)S(1)}, s32[]{:S(2)}) async-start(f32[32,8192]{1,0:T(8,128)} %param.6), calls=%async_computation.1 | async-start | bytes 32768 | tf_op jit(solution)/shard_map/slice | solution.py:90
  292.1 40.3 %copy-start.1 = (f32[32,8192]{1,0:T(8,128)S(1)}, f32[32,8192]{1,0:T(8,128)}, u32[]{:S(2)}) copy-start(f32[32,8192]{1,0:T(8,128)} %param.6) | copy-start | bytes 3145732
  553.1 36.1 %copy-start.2 = (f32[32,8192]{1,0:T(8,128)}, f32[32,8192]{1,0:T(8,128)S(1)}, u32[]{:S(2)}) copy-start(f32[32,8192]{1,0:T(8,128)S(1)} %fusion) | copy-start | bytes 3145732
Sparse Core Ops, SparseCore 0:
  362.9 113.9 all-reduce.1
